TPU v7x, 128 devices: a whole 4x4x4 slice. The times are simulated.
128 devices in a mesh: bond: 8 (over y, core), atom: 16 (over z, x).
Axes of the slice: x: 4, y: 4, z: 4, core: 2. Of those that a mesh axis runs over, the one named last changes fastest.
Arguments:
- bond_states: bfloat16 [262144, 512], P(('bond', 'atom')), may hold values from -6 to 6
- block_counts: int32 [128], P(('bond', 'atom')), may hold values from 8 to 64, as said below
- send_rows: int32 [128, 128, 64], P(('bond', 'atom')), may hold values from 0 to 2047
- source_slots: int32 [128, 2048], P(('bond', 'atom')), may hold values from 0 to 8191
- target_slots: int32 [128, 2048], P(('bond', 'atom')), may hold values from 0 to 4095
- return_rows: int32 [128, 4096], P(('bond', 'atom')), may hold values from 0 to 2047
- angular_basis: bfloat16 [8192, 32, 512], P(('bond', 'atom')), may hold values from -1 to 1
- pre_inner: bfloat16 [2, 512, 512], replicated, may hold values from -0.25 to 0.25
- pre_outer: bfloat16 [2, 512, 512], replicated, may hold values from -0.25 to 0.25
- down_proj: bfloat16 [2, 512, 64], replicated, may hold values from -0.25 to 0.25
- bilinear: bfloat16 [2, 1024, 64], replicated, may hold values from -0.1875 to 0.1875
- up_proj: bfloat16 [2, 64, 512], replicated, may hold values from -0.75 to 0.75
- post_inner: bfloat16 [2, 512, 512], replicated, may hold values from -0.25 to 0.25
- post_outer: bfloat16 [2, 512, 512], replicated, may hold values from -0.25 to 0.25
Outputs:
- bond_out: bfloat16 [262144, 512], P(('bond', 'atom'))
Inputs may be any that keep to these rules, and one draw needn't show every extreme that they name: Owner o's blocks numbered below block_counts[o] are live, the others are padding; some owner has all 64 live in every draw.
All inputs are finite; a program needn't handle non-finite values.
Results may differ from a plain program's by a relative error of at most 0.0078.
Values may be sent and summed in bfloat16 or wider, within the bound.
A program may use at most 128 MiB of HBM per device.

v0:
```python
import functools

import jax
import jax.numpy as jnp
from jax import lax
from jax.experimental import pallas as pl
from jax.experimental.pallas import tpu as pltpu
from jax.sharding import PartitionSpec as P

MESH = pl.DeviceIdType.MESH
root_half = 0.7071067811865476
bf16 = jnp.bfloat16
f32 = jnp.float32
i32 = jnp.int32


def dot(a, b):
    return jnp.dot(a, b, preferred_element_type=f32)


def silu(v):
    half = 0.5 * v
    return half * jnp.tanh(half) + half


def lanes(shape):
    return lax.broadcasted_iota(i32, shape, 1)


def one_hot(index, positions):
    return jnp.where(index == positions, 1.0, 0.0).astype(bf16)


def kernel(
    count_ref,
    x_ref,
    send_ref,
    source_ref,
    target_ref,
    target_row_ref,
    return_ref,
    return_row_ref,
    basis_ref,
    pre_in_ref,
    pre_out_ref,
    down_ref,
    bil_ref,
    up_ref,
    post_in_ref,
    post_out_ref,
    out_ref,
    inner,
    down_wide,
    up_tall,
    table,
    pick_send,
    col_send,
    pick_source,
    col_source,
    pick_target,
    col_target,
    pick_return,
    col_return,
    basis_t,
    turned,
    bil_wide,
    payload,
    arrived,
    gathered,
    mixed,
    partial,
    spread,
    outgoing,
    incoming,
    spread_in,
    message,
    send_sem,
    recv_sem,
):
    me_bond = lax.axis_index("bond")
    me_atom = lax.axis_index("atom")
    atoms = 16
    peers = 128
    me = me_bond * atoms + me_atom
    layers = 2

    barrier = pltpu.get_barrier_semaphore()

    def greet(step, carry):
        peer = lax.rem(me + step, peers)
        pl.semaphore_signal(
            barrier, inc=1, device_id=(peer // atoms, lax.rem(peer, atoms)), device_id_type=MESH
        )
        return carry

    lax.fori_loop(1, peers, greet, 0)

    lane128 = lanes((1, 128))
    low_half = lane128 < 64
    half_id = lane128 // 64
    lane256 = lanes((1, 256))
    group_id = lane256 // 64

    send_t = jnp.transpose(send_ref[...])
    for c in range(16):
        col_send[c] = send_t[:, c * 8 : (c + 1) * 8]

    def build_send(c, carry):
        cols = col_send[c]
        pos = lanes((32, 512))
        for h in range(2):
            for o in range(8):
                col = cols[h * 32 : (h + 1) * 32, o : o + 1]
                pick_send[c, h * 256 + o * 32 : h * 256 + (o + 1) * 32, :] = one_hot(col & 511, pos)
        return carry

    lax.fori_loop(0, 16, build_send, 0)

    for l in range(layers):
        for g in range(4):
            down_wide[l, :, g * 64 : (g + 1) * 64] = down_ref[l]
            up_tall[l, g * 64 : (g + 1) * 64, :] = up_ref[l]

    def residual(v, w_in, w_out):
        hidden = silu(dot(v, w_in)).astype(bf16)
        return ((v.astype(f32) + silu(dot(hidden, w_out))) * root_half).astype(bf16)

    def pre(l, g, v):
        inner_g = residual(v, pre_in_ref[l], pre_out_ref[l])
        inner[pl.ds(g * 512, 512), :] = inner_g
        proj = silu(dot(inner_g, down_wide[l])).astype(bf16)
        table[...] = jnp.where(group_id == g, proj, table[...])

    def first(g, carry):
        pre(0, g, x_ref[pl.ds(g * 512, 512), :])
        return carry

    table[...] = jnp.zeros_like(table)
    lax.fori_loop(0, 4, first, 0)

    pl.semaphore_wait(barrier, peers - 1)

    def send_block(src, dst, peer, sem_index, recv):
        @pl.when(peer != me)
        def _():
            pltpu.make_async_remote_copy(
                src_ref=src,
                dst_ref=dst,
                send_sem=send_sem.at[sem_index],
                recv_sem=recv,
                device_id=(peer // atoms, lax.rem(peer, atoms)),
                device_id_type=MESH,
            ).start()

        @pl.when(peer == me)
        def _():
            pltpu.make_async_copy(src, dst, recv).start()

    def provide(l):
        def send_chunk(c):
            for o in range(8):
                peer = c * 8 + o
                send_block(
                    payload.at[peer],
                    arrived.at[l, me // 2, lax.rem(me, 2)],
                    peer,
                    l * 2,
                    recv_sem.at[l * 8 + me // 32],
                )

        def chunk(step, carry):
            c = lax.rem(me // 8 + step, 16)
            values = dot(pick_send[c], table[...])
            cols = col_send[c]
            for o in range(8):
                half = []
                for h in range(2):
                    low = cols[h * 32 : (h + 1) * 32, o : o + 1] >> 9
                    e = values[h * 256 + o * 32 : h * 256 + (o + 1) * 32]
                    v = jnp.where(low >= 2, e[:, 128:], e[:, :128])
                    half.append((v, pltpu.roll(v, 64, 1), (low & 1) == 1))
                (v0, w0, odd0), (v1, w1, odd1) = half
                picked = jnp.where(low_half, jnp.where(odd0, w0, v0), jnp.where(odd1, v1, w1))
                payload[c * 8 + o] = picked.astype(bf16)

            @pl.when(step > 0)
            def _():
                send_chunk(lax.rem(me // 8 + step + 15, 16))

            return carry

        lax.fori_loop(0, 16, chunk, 0)
        send_chunk(lax.rem(me // 8 + 15, 16))

    def prepare():
        source_t = jnp.transpose(source_ref[...])
        target_t = jnp.transpose(target_ref[...])
        return_t = jnp.transpose(return_ref[...])
        rows = lax.broadcasted_iota(i32, (128, 1), 0) // 32
        for c in range(16):
            col_source[c] = source_t[:, c : c + 1]
            t = target_t[:, c : c + 1]
            low = ((t >> 5) & 1) * 2 + ((t >> 4) & 1)
            col_target[c] = jnp.where(rows + c * 4 < count_ref[0], low, -1)
        for c in range(32):
            col_return[c] = return_t[:, c : c + 1] >> 9

        def build_source(c, carry):
            s = col_source[c]
            key = (s >> 7) * 32 + (s & 31)
            for k in range(4):
                pick_source[k, pl.ds(c * 128, 128), :] = one_hot(key, lanes((128, 512)) + k * 512)
            return carry

        lax.fori_loop(0, 16, build_source, 0)

        t = target_row_ref[...]
        target_key = (t >> 6) * 16 + (t & 15)

        def build_target(c, carry):
            pos = lax.broadcasted_iota(i32, (64, 2048), 0) + c * 64
            pick_target[pl.ds(c * 64, 64), :] = one_hot(target_key, pos)
            return carry

        lax.fori_loop(0, 16, build_target, 0)

        return_key = return_row_ref[...] & 511

        def build_return(c, carry):
            pos = lax.broadcasted_iota(i32, (64, 1024), 0) + c * 64
            for k in range(4):
                key = return_key[:, k * 1024 : (k + 1) * 1024]
                pick_return[k, pl.ds(c * 64, 64), :] = one_hot(key, pos)
            return carry

        lax.fori_loop(0, 8, build_return, 0)

        def turn(g, carry):
            block = basis_ref[pl.ds(g * 4, 4)].reshape(128, 512).astype(f32)
            turned[...] = jnp.transpose(block)
            for k in range(16):
                basis_t[g, k * 32 : (k + 1) * 32, :] = turned[pl.ds(k, 32, stride=16), :].astype(bf16)
            return carry

        lax.fori_loop(0, 16, turn, 0)

        bil_wide[...] = jnp.zeros_like(bil_wide)
        for l in range(layers):

            def widen(k, carry):
                w = bil_ref[l, pl.ds(k * 64, 64), :]
                for b in range(4):
                    bil_wide[l, pl.ds(k * 256 + b * 64, 64), b * 64 : (b + 1) * 64] = w
                return carry

            lax.fori_loop(0, 16, widen, 0)

    def triplet(l):
        for n in range(4):
            k = lax.rem(me // 32 + 4 - n, 4)
            pltpu.make_async_copy(
                arrived.at[l, pl.ds(0, 16)], arrived.at[l, pl.ds(0, 16)], recv_sem.at[l * 8 + k]
            ).wait()
            block = jnp.concatenate(
                [
                    arrived[l, pl.ds(k * 16, 16), 0].reshape(512, 128),
                    arrived[l, pl.ds(k * 16, 16), 1].reshape(512, 128),
                ],
                axis=1,
            )

            def gather(m, carry):
                part = dot(pick_source[k, pl.ds(m * 512, 512), :], block)
                if n > 0:
                    part = part + gathered[pl.ds(m * 512, 512), :]
                gathered[pl.ds(m * 512, 512), :] = part
                return carry

            lax.fori_loop(0, 4, gather, 0)

        row_block = lax.broadcasted_iota(i32, (128, 1), 0) // 32

        def contract(g, carry):
            s = col_source[g]
            a = gathered[pl.ds(g * 128, 128), :]
            v = jnp.where(((s >> 6) & 1) == 1, a[:, 128:], a[:, :128])
            w = pltpu.roll(v, 64, 1)
            both = jnp.where(((s >> 5) & 1) != half_id, w, v)
            right = jnp.concatenate(
                [
                    jnp.where(row_block == half_id, both, 0.0),
                    jnp.where(row_block == half_id + 2, both, 0.0),
                ],
                axis=1,
            ).astype(bf16)
            c = dot(basis_t[g], right).astype(bf16)
            for k in range(16):
                mixed[pl.ds(g * 32, 32), k * 256 : (k + 1) * 256] = c[k * 32 : (k + 1) * 32]
            return carry

        lax.fori_loop(0, 16, contract, 0)

        partial[...] = dot(mixed[...], bil_wide[l])

        def scatter(g, carry):
            p = partial[pl.ds(g * 32, 32), :]
            for half in range(2):
                v = p[:, half * 128 : (half + 1) * 128]
                w = pltpu.roll(v, 64, 1)
                for b in range(2):
                    both = jnp.where(low_half, v, w) if b == 0 else jnp.where(low_half, w, v)
                    b4 = half * 2 + b
                    low = col_target[g, b4 * 32 : (b4 + 1) * 32, :]
                    rows = pl.ds(g * 128 + b4 * 32, 32)
                    spread[rows, 0:128] = jnp.where(low == half_id, both, 0.0).astype(bf16)
                    spread[rows, 128:256] = jnp.where(low == half_id + 2, both, 0.0).astype(bf16)
            return carry

        lax.fori_loop(0, 16, scatter, 0)

    def give_back(l):
        def send_chunk(c):
            def one(i, carry):
                peer = c * 32 + i
                send_block(
                    outgoing.at[peer // 2, lax.rem(peer, 2)],
                    incoming.at[l, me],
                    peer,
                    l * 2 + 1,
                    recv_sem.at[l * 8 + 4 + me // 32],
                )
                return carry

            lax.fori_loop(0, 32, one, 0)

        def chunk(n, carry):
            c = lax.rem(me // 32 + n, 4)
            sums = dot(pick_target[pl.ds(c * 256, 256), :], spread[...]).astype(bf16)
            outgoing[pl.ds(c * 16, 16), 0] = sums[:, :128].reshape(16, 16, 128)
            outgoing[pl.ds(c * 16, 16), 1] = sums[:, 128:].reshape(16, 16, 128)

            @pl.when(n > 0)
            def _():
                send_chunk(lax.rem(me // 32 + n + 3, 4))

            return carry

        lax.fori_loop(0, 4, chunk, 0)
        send_chunk(lax.rem(me // 32 + 3, 4))

    def receive(l):
        for n in range(4):
            c = lax.rem(me // 32 + 4 - n, 4)
            pltpu.make_async_copy(
                incoming.at[l, pl.ds(0, 32)], incoming.at[l, pl.ds(0, 32)], recv_sem.at[l * 8 + 4 + c]
            ).wait()

            def place(q, carry):
                for o in range(4):
                    v = incoming[l, c * 32 + q * 4 + o].astype(f32)
                    w = pltpu.roll(v, 64, 1)
                    for h in range(2):
                        both = jnp.where(low_half, v, w) if h == 0 else jnp.where(low_half, w, v)
                        low = col_return[c * 8 + q, o * 32 + h * 16 : o * 32 + (h + 1) * 16, :]
                        rows = pl.ds(q * 128 + o * 32 + h * 16, 16)
                        spread_in[rows, 0:128] = jnp.where(low == half_id, both, 0.0).astype(bf16)
                        spread_in[rows, 128:256] = jnp.where(low == half_id + 2, both, 0.0).astype(bf16)
                return carry

            lax.fori_loop(0, 8, place, 0)
            part = dot(pick_return[c], spread_in[...])
            if n > 0:
                part = part + message[...]
            message[...] = part

    def post(l, g):
        picked = jnp.where(group_id == g, message[...], 0.0).astype(bf16)
        added = silu(dot(picked, up_tall[l]))
        joined = ((inner[pl.ds(g * 512, 512), :].astype(f32) + added) * root_half).astype(bf16)
        return residual(joined, post_in_ref[l], post_out_ref[l])

    def sent(rows, index):
        pltpu.make_async_copy(rows, rows, send_sem.at[index]).wait()

    for l in range(layers):
        provide(l)
        if l == 0:
            prepare()
        triplet(l)
        sent(payload.at[pl.ds(0, peers - 1)], l * 2)
        give_back(l)
        receive(l)
        sent(incoming.at[l, pl.ds(0, peers - 1)], l * 2 + 1)
        if l < layers - 1:

            def middle(g, carry):
                pre(l + 1, g, post(l, g))
                return carry

            lax.fori_loop(0, 4, middle, 0)
        else:

            def last(g, carry):
                out_ref[pl.ds(g * 512, 512), :] = post(l, g)
                return carry

            lax.fori_loop(0, 4, last, 0)


def on_device(
    bond_states,
    block_counts,
    send_rows,
    source_slots,
    target_slots,
    return_rows,
    angular_basis,
    pre_inner,
    pre_outer,
    down_proj,
    bilinear,
    up_proj,
    post_inner,
    post_outer,
):
    vmem = pl.BlockSpec(memory_space=pltpu.VMEM)
    return pl.pallas_call(
        kernel,
        name="triplet",
        out_shape=jax.ShapeDtypeStruct((2048, 512), bf16),
        in_specs=[pl.BlockSpec(memory_space=pltpu.SMEM)] + [vmem] * 15,
        out_specs=vmem,
        scratch_shapes=[
            pltpu.VMEM((2048, 512), bf16),
            pltpu.VMEM((2, 512, 256), bf16),
            pltpu.VMEM((2, 256, 512), bf16),
            pltpu.VMEM((512, 256), bf16),
            pltpu.VMEM((16, 512, 512), bf16),
            pltpu.VMEM((16, 64, 8), i32),
            pltpu.VMEM((4, 2048, 512), bf16),
            pltpu.VMEM((16, 128, 1), i32),
            pltpu.VMEM((1024, 2048), bf16),
            pltpu.VMEM((16, 128, 1), i32),
            pltpu.VMEM((4, 512, 1024), bf16),
            pltpu.VMEM((32, 128, 1), i32),
            pltpu.VMEM((16, 512, 128), bf16),
            pltpu.VMEM((512, 128), f32),
            pltpu.VMEM((2, 4096, 256), bf16),
            pltpu.VMEM((128, 32, 128), bf16),
            pltpu.VMEM((2, 64, 2, 32, 128), bf16),
            pltpu.VMEM((2048, 256), f32),
            pltpu.VMEM((512, 4096), bf16),
            pltpu.VMEM((512, 256), f32),
            pltpu.VMEM((2048, 256), bf16),
            pltpu.VMEM((64, 2, 16, 128), bf16),
            pltpu.VMEM((2, 128, 16, 128), bf16),
            pltpu.VMEM((1024, 256), bf16),
            pltpu.VMEM((512, 256), f32),
            pltpu.SemaphoreType.DMA((4,)),
            pltpu.SemaphoreType.DMA((16,)),
        ],
        compiler_params=pltpu.CompilerParams(
            collective_id=0, has_side_effects=True, vmem_limit_bytes=67043328
        ),
    )(
        block_counts,
        bond_states,
        send_rows[0],
        source_slots.reshape(16, 128),
        target_slots.reshape(16, 128),
        target_slots,
        return_rows.reshape(32, 128),
        return_rows,
        angular_basis,
        pre_inner,
        pre_outer,
        down_proj,
        bilinear,
        up_proj,
        post_inner,
        post_outer,
    )


def solution(mesh):
    split = ("bond", "atom")
    in_specs = (
        P(split, None),
        P(split),
        P(split, None, None),
        P(split, None),
        P(split, None),
        P(split, None),
        P(split, None, None),
    ) + (P(),) * 7
    return jax.shard_map(
        on_device, mesh=mesh, in_specs=in_specs, out_specs=P(split, None), check_vma=False
    )
```

profile of v0, /device:TPU:1, one launch (start us, length us, event | category | flops | bytes accessed | tf_op | source)
XLA Modules:
  0.0 132.1 jit_solution(15135546811622481484)
XLA Ops:
  0.7 1.5 %copy.15 = s32[1,128,64]{2,1,0:T(8,128)} copy(s32[1,128,64]{1,2,0:T(8,128)} %param.16) | data formatting | bytes 65536 | tf_op args[2]
  2.1 1.8 %copy.16.down_ref = bf16[2,512,64]{2,1,0:T(8,128)(2,1)} copy(bf16[2,512,64]{1,2,0:T(8,128)(2,1)} %param.23) | data formatting | bytes 262144 | tf_op args[9]
  3.9 2.0 %copy.17.bil_ref = bf16[2,1024,64]{2,1,0:T(8,128)(2,1)} copy(bf16[2,1024,64]{1,2,0:T(8,128)(2,1)} %param.24) | data formatting | bytes 524288 | tf_op args[10]
  5.8 123.2 %triplet.1 = bf16[2048,512]{1,0:T(8,128)(2,1)} custom-call(s32[1]{0:T(128)S(6)} %copy.19.count_ref, bf16[2048,512]{1,0:T(8,128)(2,1)} %x_ref.1, s32[128,64]{1,0:T(8,128)} %bitcast.4, s32[16,128]{1,0:T(8,128)} %bitcast.7, s32[16,128]{1,0:T(8,128)} %bitcast.6, s32[1,2048]{1,0:T(1,128)} %target_row_ref.1, s32[32,128]{1,0:T(8,128)} %bitcast.5, ...), custom_call_target="tpu_custom_call" | custom-call | tf_op jit(solution)/shard_map/triplet/pallas_call | solution.py:427
  129.0 3.0 %copy.20 = bf16[2048,512]{1,0:T(8,128)(2,1)} copy(bf16[2048,512]{1,0:T(8,128)(2,1)} %triplet.1) | data formatting | bytes 4194304
where the time goes:
time: 133 us; the launch traced here: 132 us
  Pallas kernels  123 us (92%)
  local copies, waits for them, and re-layouts  8.24 us (6%)
    pallas_call x1, Pallas kernels, on_device(): pl.pallas_call(kernel, name='triplet', out_shape=jax.ShapeDtypeStruct((20...  123 us
    unnamed x4, local copies, waits for them, and re-layouts  8.24 us

commit v1 on v0

--- a/solution.py
+++ b/solution.py
@@ -31,15 +31,55 @@
     return jnp.where(index == positions, 1.0, 0.0).astype(bf16)
 
 
+def loop(count, unroll, body):
+    def some(step, carry):
+        for u in range(unroll):
+            body(step * unroll + u)
+        return carry
+
+    if count == unroll:
+        some(0, 0)
+    else:
+        lax.fori_loop(0, count // unroll, some, 0)
+
+
+def residual(v, w_in, w_out):
+    hidden = silu(dot(v, w_in)).astype(bf16)
+    return ((v.astype(f32) + silu(dot(hidden, w_out))) * root_half).astype(bf16)
+
+
+def join(g, inner_g, message, up_tall):
+    group_id = lanes((1, 256)) // 64
+    picked = jnp.where(group_id == g, message, jnp.zeros_like(message))
+    added = silu(dot(picked, up_tall))
+    return ((inner_g.astype(f32) + added) * root_half).astype(bf16)
+
+
+def final(inner_ref, message_ref, up_ref, w_in_ref, w_out_ref, out_ref):
+    up_tall = jnp.concatenate([up_ref[0]] * 4, axis=0)
+    joined = join(pl.program_id(0), inner_ref[...], message_ref[...], up_tall)
+    out_ref[...] = residual(joined, w_in_ref[0], w_out_ref[0])
+
+
 def kernel(
     count_ref,
-    x_ref,
     send_ref,
     source_ref,
     target_ref,
     target_row_ref,
     return_ref,
     return_row_ref,
+    x_hbm,
+    basis_hbm,
+    pre_in_hbm,
+    pre_out_hbm,
+    down_hbm,
+    bil_hbm,
+    up_hbm,
+    post_in_hbm,
+    post_out_hbm,
+    inner_hbm,
+    message_ref,
     basis_ref,
     pre_in_ref,
     pre_out_ref,
@@ -48,7 +88,6 @@
     up_ref,
     post_in_ref,
     post_out_ref,
-    out_ref,
     inner,
     down_wide,
     up_tall,
@@ -76,6 +115,7 @@
     message,
     send_sem,
     recv_sem,
+    load_sem,
 ):
     me_bond = lax.axis_index("bond")
     me_atom = lax.axis_index("atom")
@@ -95,35 +135,50 @@
 
     lax.fori_loop(1, peers, greet, 0)
 
+    loads = [
+        pltpu.make_async_copy(src, dst, load_sem.at[n])
+        for n, (src, dst) in enumerate(
+            (
+                (down_hbm, down_ref),
+                (pre_in_hbm, pre_in_ref),
+                (pre_out_hbm, pre_out_ref),
+                (x_hbm, inner),
+                (basis_hbm, basis_ref),
+                (bil_hbm, bil_ref),
+                (up_hbm, up_ref),
+                (post_in_hbm.at[0], post_in_ref),
+                (post_out_hbm.at[0], post_out_ref),
+            )
+        )
+    ]
+    for copy in loads:
+        copy.start()
+    store = pltpu.make_async_copy(inner, inner_hbm, load_sem.at[len(loads)])
+
     lane128 = lanes((1, 128))
     low_half = lane128 < 64
     half_id = lane128 // 64
     lane256 = lanes((1, 256))
     group_id = lane256 // 64
 
-    send_t = jnp.transpose(send_ref[...])
     for c in range(16):
-        col_send[c] = send_t[:, c * 8 : (c + 1) * 8]
-
-    def build_send(c, carry):
+        col_send[c] = send_ref[:, c * 8 : (c + 1) * 8]
+
+    def build_send(c):
         cols = col_send[c]
         pos = lanes((32, 512))
         for h in range(2):
             for o in range(8):
                 col = cols[h * 32 : (h + 1) * 32, o : o + 1]
                 pick_send[c, h * 256 + o * 32 : h * 256 + (o + 1) * 32, :] = one_hot(col & 511, pos)
-        return carry
-
-    lax.fori_loop(0, 16, build_send, 0)
-
+
+    loop(16, 1, build_send)
+
+    loads[0].wait()
     for l in range(layers):
+        down = jnp.transpose(down_ref[l].astype(f32)).astype(bf16)
         for g in range(4):
-            down_wide[l, :, g * 64 : (g + 1) * 64] = down_ref[l]
-            up_tall[l, g * 64 : (g + 1) * 64, :] = up_ref[l]
-
-    def residual(v, w_in, w_out):
-        hidden = silu(dot(v, w_in)).astype(bf16)
-        return ((v.astype(f32) + silu(dot(hidden, w_out))) * root_half).astype(bf16)
+            down_wide[l, :, g * 64 : (g + 1) * 64] = down
 
     def pre(l, g, v):
         inner_g = residual(v, pre_in_ref[l], pre_out_ref[l])
@@ -131,12 +186,13 @@
         proj = silu(dot(inner_g, down_wide[l])).astype(bf16)
         table[...] = jnp.where(group_id == g, proj, table[...])
 
-    def first(g, carry):
-        pre(0, g, x_ref[pl.ds(g * 512, 512), :])
-        return carry
+    def first(g):
+        pre(0, g, inner[pl.ds(g * 512, 512), :])
 
     table[...] = jnp.zeros_like(table)
-    lax.fori_loop(0, 4, first, 0)
+    for copy in loads[1:4]:
+        copy.wait()
+    loop(4, 1, first)
 
     pl.semaphore_wait(barrier, peers - 1)
 
@@ -158,7 +214,7 @@
 
     def provide(l):
         def send_chunk(c):
-            for o in range(8):
+            def one(o, carry):
                 peer = c * 8 + o
                 send_block(
                     payload.at[peer],
@@ -167,9 +223,11 @@
                     l * 2,
                     recv_sem.at[l * 8 + me // 32],
                 )
-
-        def chunk(step, carry):
-            c = lax.rem(me // 8 + step, 16)
+                return carry
+
+            lax.fori_loop(0, 8, one, 0)
+
+        def compute(c):
             values = dot(pick_send[c], table[...])
             cols = col_send[c]
             for o in range(8):
@@ -183,77 +241,86 @@
                 picked = jnp.where(low_half, jnp.where(odd0, w0, v0), jnp.where(odd1, v1, w1))
                 payload[c * 8 + o] = picked.astype(bf16)
 
+        def chunk(step, carry):
+            for u in range(2):
+                compute(lax.rem(me // 8 + step * 2 + u, 16))
+
             @pl.when(step > 0)
             def _():
-                send_chunk(lax.rem(me // 8 + step + 15, 16))
+                for u in range(2):
+                    send_chunk(lax.rem(me // 8 + step * 2 + u + 14, 16))
 
             return carry
 
-        lax.fori_loop(0, 16, chunk, 0)
-        send_chunk(lax.rem(me // 8 + 15, 16))
+        lax.fori_loop(0, 8, chunk, 0)
+        for u in range(2):
+            send_chunk(lax.rem(me // 8 + 14 + u, 16))
 
     def prepare():
         source_t = jnp.transpose(source_ref[...])
         target_t = jnp.transpose(target_ref[...])
-        return_t = jnp.transpose(return_ref[...])
         rows = lax.broadcasted_iota(i32, (128, 1), 0) // 32
         for c in range(16):
             col_source[c] = source_t[:, c : c + 1]
             t = target_t[:, c : c + 1]
             low = ((t >> 5) & 1) * 2 + ((t >> 4) & 1)
             col_target[c] = jnp.where(rows + c * 4 < count_ref[0], low, -1)
-        for c in range(32):
-            col_return[c] = return_t[:, c : c + 1] >> 9
-
-        def build_source(c, carry):
+
+        def build_source(c):
             s = col_source[c]
             key = (s >> 7) * 32 + (s & 31)
             for k in range(4):
                 pick_source[k, pl.ds(c * 128, 128), :] = one_hot(key, lanes((128, 512)) + k * 512)
-            return carry
-
-        lax.fori_loop(0, 16, build_source, 0)
+
+        loop(16, 1, build_source)
 
         t = target_row_ref[...]
         target_key = (t >> 6) * 16 + (t & 15)
 
-        def build_target(c, carry):
+        def build_target(c):
             pos = lax.broadcasted_iota(i32, (64, 2048), 0) + c * 64
             pick_target[pl.ds(c * 64, 64), :] = one_hot(target_key, pos)
-            return carry
-
-        lax.fori_loop(0, 16, build_target, 0)
-
+
+        loop(16, 1, build_target)
+
+        loads[4].wait()
+
+        def turn(g):
+            block = basis_ref[pl.ds(g * 4, 4)].reshape(128, 512).astype(f32)
+            turned[...] = jnp.transpose(block)
+            for k in range(16):
+                basis_t[g, k * 32 : (k + 1) * 32, :] = turned[pl.ds(k, 32, stride=16), :].astype(bf16)
+
+        loop(16, 1, turn)
+
+        loads[5].wait()
+        bil_wide[...] = jnp.zeros_like(bil_wide)
+        for l in range(layers):
+            for k in range(16):
+                if k % 2 == 0:
+                    pair = jnp.transpose(bil_ref[l, :, k * 64 : k * 64 + 128].astype(f32)).astype(bf16)
+                w = pair[k % 2 * 64 : k % 2 * 64 + 64]
+                for b in range(4):
+                    start = k * 256 + b * 64
+                    bil_wide[l, start : start + 64, b * 64 : (b + 1) * 64] = w
+
+    def prepare_return():
+        return_t = jnp.transpose(return_ref[...])
+        for c in range(32):
+            col_return[c] = return_t[:, c : c + 1] >> 9
         return_key = return_row_ref[...] & 511
 
-        def build_return(c, carry):
+        def build_return(c):
             pos = lax.broadcasted_iota(i32, (64, 1024), 0) + c * 64
             for k in range(4):
                 key = return_key[:, k * 1024 : (k + 1) * 1024]
                 pick_return[k, pl.ds(c * 64, 64), :] = one_hot(key, pos)
-            return carry
-
-        lax.fori_loop(0, 8, build_return, 0)
-
-        def turn(g, carry):
-            block = basis_ref[pl.ds(g * 4, 4)].reshape(128, 512).astype(f32)
-            turned[...] = jnp.transpose(block)
-            for k in range(16):
-                basis_t[g, k * 32 : (k + 1) * 32, :] = turned[pl.ds(k, 32, stride=16), :].astype(bf16)
-            return carry
-
-        lax.fori_loop(0, 16, turn, 0)
-
-        bil_wide[...] = jnp.zeros_like(bil_wide)
-        for l in range(layers):
-
-            def widen(k, carry):
-                w = bil_ref[l, pl.ds(k * 64, 64), :]
-                for b in range(4):
-                    bil_wide[l, pl.ds(k * 256 + b * 64, 64), b * 64 : (b + 1) * 64] = w
-                return carry
-
-            lax.fori_loop(0, 16, widen, 0)
+
+        loop(8, 1, build_return)
+        for copy in loads[6:]:
+            copy.wait()
+        for g in range(4):
+            up_tall[g * 64 : (g + 1) * 64, :] = up_ref[0]
 
     def triplet(l):
         for n in range(4):
@@ -269,18 +336,17 @@
                 axis=1,
             )
 
-            def gather(m, carry):
-                part = dot(pick_source[k, pl.ds(m * 512, 512), :], block)
+            def gather(m):
+                part = dot(pick_source[k, pl.ds(m * 1024, 1024), :], block)
                 if n > 0:
-                    part = part + gathered[pl.ds(m * 512, 512), :]
-                gathered[pl.ds(m * 512, 512), :] = part
-                return carry
-
-            lax.fori_loop(0, 4, gather, 0)
+                    part = part + gathered[pl.ds(m * 1024, 1024), :]
+                gathered[pl.ds(m * 1024, 1024), :] = part
+
+            loop(2, 1, gather)
 
         row_block = lax.broadcasted_iota(i32, (128, 1), 0) // 32
 
-        def contract(g, carry):
+        def contract(g):
             s = col_source[g]
             a = gathered[pl.ds(g * 128, 128), :]
             v = jnp.where(((s >> 6) & 1) == 1, a[:, 128:], a[:, :128])
@@ -296,13 +362,12 @@
             c = dot(basis_t[g], right).astype(bf16)
             for k in range(16):
                 mixed[pl.ds(g * 32, 32), k * 256 : (k + 1) * 256] = c[k * 32 : (k + 1) * 32]
-            return carry
-
-        lax.fori_loop(0, 16, contract, 0)
+
+        loop(16, 4, contract)
 
         partial[...] = dot(mixed[...], bil_wide[l])
 
-        def scatter(g, carry):
+        def scatter(g):
             p = partial[pl.ds(g * 32, 32), :]
             for half in range(2):
                 v = p[:, half * 128 : (half + 1) * 128]
@@ -314,9 +379,8 @@
                     rows = pl.ds(g * 128 + b4 * 32, 32)
                     spread[rows, 0:128] = jnp.where(low == half_id, both, 0.0).astype(bf16)
                     spread[rows, 128:256] = jnp.where(low == half_id + 2, both, 0.0).astype(bf16)
-            return carry
-
-        lax.fori_loop(0, 16, scatter, 0)
+
+        loop(16, 4, scatter)
 
     def give_back(l):
         def send_chunk(c):
@@ -355,7 +419,7 @@
                 incoming.at[l, pl.ds(0, 32)], incoming.at[l, pl.ds(0, 32)], recv_sem.at[l * 8 + 4 + c]
             ).wait()
 
-            def place(q, carry):
+            def place(q):
                 for o in range(4):
                     v = incoming[l, c * 32 + q * 4 + o].astype(f32)
                     w = pltpu.roll(v, 64, 1)
@@ -365,19 +429,12 @@
                         rows = pl.ds(q * 128 + o * 32 + h * 16, 16)
                         spread_in[rows, 0:128] = jnp.where(low == half_id, both, 0.0).astype(bf16)
                         spread_in[rows, 128:256] = jnp.where(low == half_id + 2, both, 0.0).astype(bf16)
-                return carry
-
-            lax.fori_loop(0, 8, place, 0)
+
+            loop(8, 4, place)
             part = dot(pick_return[c], spread_in[...])
             if n > 0:
                 part = part + message[...]
             message[...] = part
-
-    def post(l, g):
-        picked = jnp.where(group_id == g, message[...], 0.0).astype(bf16)
-        added = silu(dot(picked, up_tall[l]))
-        joined = ((inner[pl.ds(g * 512, 512), :].astype(f32) + added) * root_half).astype(bf16)
-        return residual(joined, post_in_ref[l], post_out_ref[l])
 
     def sent(rows, index):
         pltpu.make_async_copy(rows, rows, send_sem.at[index]).wait()
@@ -389,22 +446,22 @@
         triplet(l)
         sent(payload.at[pl.ds(0, peers - 1)], l * 2)
         give_back(l)
+        if l == 0:
+            prepare_return()
         receive(l)
         sent(incoming.at[l, pl.ds(0, peers - 1)], l * 2 + 1)
         if l < layers - 1:
-
-            def middle(g, carry):
-                pre(l + 1, g, post(l, g))
-                return carry
-
-            lax.fori_loop(0, 4, middle, 0)
+            message_ref[...] = message[...].astype(bf16)
+
+            def middle(g):
+                joined = join(g, inner[pl.ds(g * 512, 512), :], message_ref[...], up_tall[...])
+                pre(l + 1, g, residual(joined, post_in_ref[...], post_out_ref[...]))
+
+            loop(4, 1, middle)
+            store.start()
         else:
-
-            def last(g, carry):
-                out_ref[pl.ds(g * 512, 512), :] = post(l, g)
-                return carry
-
-            lax.fori_loop(0, 4, last, 0)
+            message_ref[...] = message[...].astype(bf16)
+    store.wait()
 
 
 def on_device(
@@ -424,16 +481,28 @@
     post_outer,
 ):
     vmem = pl.BlockSpec(memory_space=pltpu.VMEM)
-    return pl.pallas_call(
+    hbm = pl.BlockSpec(memory_space=pl.ANY)
+    inner, message = pl.pallas_call(
         kernel,
         name="triplet",
-        out_shape=jax.ShapeDtypeStruct((2048, 512), bf16),
-        in_specs=[pl.BlockSpec(memory_space=pltpu.SMEM)] + [vmem] * 15,
-        out_specs=vmem,
+        out_shape=(
+            jax.ShapeDtypeStruct((2048, 512), bf16),
+            jax.ShapeDtypeStruct((512, 256), bf16),
+        ),
+        in_specs=[pl.BlockSpec(memory_space=pltpu.SMEM)] + [vmem] * 6 + [hbm] * 9,
+        out_specs=(hbm, vmem),
         scratch_shapes=[
+            pltpu.VMEM((64, 32, 512), bf16),
+            pltpu.VMEM((2, 512, 512), bf16),
+            pltpu.VMEM((2, 512, 512), bf16),
+            pltpu.VMEM((2, 64, 512), bf16),
+            pltpu.VMEM((2, 64, 1024), bf16),
+            pltpu.VMEM((2, 64, 512), bf16),
+            pltpu.VMEM((512, 512), bf16),
+            pltpu.VMEM((512, 512), bf16),
             pltpu.VMEM((2048, 512), bf16),
             pltpu.VMEM((2, 512, 256), bf16),
-            pltpu.VMEM((2, 256, 512), bf16),
+            pltpu.VMEM((256, 512), bf16),
             pltpu.VMEM((512, 256), bf16),
             pltpu.VMEM((16, 512, 512), bf16),
             pltpu.VMEM((16, 64, 8), i32),
@@ -458,28 +527,44 @@
             pltpu.VMEM((512, 256), f32),
             pltpu.SemaphoreType.DMA((4,)),
             pltpu.SemaphoreType.DMA((16,)),
+            pltpu.SemaphoreType.DMA((10,)),
         ],
         compiler_params=pltpu.CompilerParams(
             collective_id=0, has_side_effects=True, vmem_limit_bytes=67043328
         ),
     )(
         block_counts,
-        bond_states,
-        send_rows[0],
+        jnp.transpose(send_rows[0]),
         source_slots.reshape(16, 128),
         target_slots.reshape(16, 128),
         target_slots,
         return_rows.reshape(32, 128),
         return_rows,
+        bond_states,
         angular_basis,
         pre_inner,
         pre_outer,
-        down_proj,
-        bilinear,
+        jnp.swapaxes(down_proj, 1, 2),
+        jnp.swapaxes(bilinear, 1, 2),
         up_proj,
         post_inner,
         post_outer,
     )
+    last = pl.BlockSpec((1, 512, 512), lambda g: (1, 0, 0))
+    return pl.pallas_call(
+        final,
+        name="final",
+        grid=(4,),
+        out_shape=jax.ShapeDtypeStruct((2048, 512), bf16),
+        in_specs=[
+            pl.BlockSpec((512, 512), lambda g: (g, 0)),
+            pl.BlockSpec((512, 256), lambda g: (0, 0)),
+            pl.BlockSpec((1, 64, 512), lambda g: (1, 0, 0)),
+            last,
+            last,
+        ],
+        out_specs=pl.BlockSpec((512, 512), lambda g: (g, 0)),
+    )(inner, message, up_proj, post_inner, post_outer)
 
 
 def solution(mesh):

time: 133 us -> 109 us (0.82)
  Pallas kernels: 123 us -> 108 us
  local copies, waits for them, and re-layouts: 8.24 us -> 0 us
    pallas_call x1 -> x2, Pallas kernels: 123 us -> 108 us  [the longest x1 101 us: on_device(): pl.pallas_call(kernel, name='triplet', out_shape=(jax.ShapeDtypeStruct((2...]
    unnamed x4 -> x0, local copies, waits for them, and re-layouts: 8.24 us -> none
where the time goes in v1:
time: 109 us
  Pallas kernels  108 us (99%)
    pallas_call x1, Pallas kernels, on_device(): pl.pallas_call(kernel, name='triplet', out_shape=(jax.ShapeDtypeStruct((2...  101 us
    pallas_call x1, Pallas kernels, on_device(): pl.pallas_call(final, name='final', grid=(4,), out_shape=jax.ShapeDtypeSt...  7.37 us

profile of v1, /device:TPU:1, one launch (start us, length us, event | category | flops | bytes accessed | tf_op | source)
XLA Modules:
  0.0 108.7 jit_solution(852965030001667557)
XLA Ops:
  0.7 100.7 %triplet.1 = (bf16[2048,512]{1,0:T(8,128)(2,1)}, bf16[512,256]{1,0:T(8,128)(2,1)}) custom-call(s32[1]{0:T(128)S(6)} %copy.15.count_ref, s32[64,128]{1,0:T(8,128)} %bitcast.11, s32[16,128]{1,0:T(8,128)} %bitcast.13, s32[16,128]{1,0:T(8,128)} %bitcast.12, s32[1,2048]{1,0:T(1,128)} %target_row_ref.1, s32[32,128]{1,0:T(8,128)} %bitcast.10, ...), custom_call_target="tpu_custom_call" | custom-call | tf_op jit(solution)/shard_map/triplet/pallas_call | solution.py:485
  101.3 7.4 %final.1 = bf16[2048,512]{1,0:T(8,128)(2,1)} custom-call(bf16[2048,512]{1,0:T(8,128)(2,1)} %get-tuple-element.7.inner_ref, bf16[512,256]{1,0:T(8,128)(2,1)} %get-tuple-element.8.message_ref, bf16[2,64,512]{2,1,0:T(8,128)(2,1)} %up_ref.1, bf16[2,512,512]{2,1,0:T(8,128)(2,1)} %w_in_ref.1, bf16[2,512,512]{2,1,0:T(8,128)(2,1)} %w_out_ref.1), custom_call_target="tpu_custom_call" | custom-call | tf_op jit(solution)/shard_map/final/pallas_call | solution.py:554

commit v2 on v1

--- a/solution.py
+++ b/solution.py
@@ -215,7 +215,7 @@
     def provide(l):
         def send_chunk(c):
             def one(o, carry):
-                peer = c * 8 + o
+                peer = c * 8 + lax.rem(me + o, 8)
                 send_block(
                     payload.at[peer],
                     arrived.at[l, me // 2, lax.rem(me, 2)],
@@ -363,7 +363,7 @@
             for k in range(16):
                 mixed[pl.ds(g * 32, 32), k * 256 : (k + 1) * 256] = c[k * 32 : (k + 1) * 32]
 
-        loop(16, 4, contract)
+        loop(16, 8, contract)
 
         partial[...] = dot(mixed[...], bil_wide[l])
 
@@ -385,7 +385,7 @@
     def give_back(l):
         def send_chunk(c):
             def one(i, carry):
-                peer = c * 32 + i
+                peer = c * 32 + lax.rem(me + i, 32)
                 send_block(
                     outgoing.at[peer // 2, lax.rem(peer, 2)],
                     incoming.at[l, me],

time: 109 us -> 108 us (level)
    pallas_call x1, Pallas kernels: 101 us -> 99.5 us  [on_device(): pl.pallas_call(kernel, name='triplet', out_shape=(jax.ShapeDtypeStruct((2...]
where the time goes in v2:
time: 108 us; the launch traced here: 107 us
  Pallas kernels  107 us (99%)
    pallas_call x1, Pallas kernels, on_device(): pl.pallas_call(kernel, name='triplet', out_shape=(jax.ShapeDtypeStruct((2...  99.5 us
    pallas_call x1, Pallas kernels, on_device(): pl.pallas_call(final, name='final', grid=(4,), out_shape=jax.ShapeDtypeSt...  7.37 us

profile of v2, /device:TPU:1, one launch (start us, length us, event | category | flops | bytes accessed | tf_op | source)
XLA Modules:
  0.0 107.5 jit_solution(8710521243744473767)
XLA Ops:
  0.7 99.5 %triplet.1 = (bf16[2048,512]{1,0:T(8,128)(2,1)}, bf16[512,256]{1,0:T(8,128)(2,1)}) custom-call(s32[1]{0:T(128)S(6)} %copy.15.count_ref, s32[64,128]{1,0:T(8,128)} %bitcast.11, s32[16,128]{1,0:T(8,128)} %bitcast.13, s32[16,128]{1,0:T(8,128)} %bitcast.12, s32[1,2048]{1,0:T(1,128)} %target_row_ref.1, s32[32,128]{1,0:T(8,128)} %bitcast.10, ...), custom_call_target="tpu_custom_call" | custom-call | tf_op jit(solution)/shard_map/triplet/pallas_call | solution.py:485
  100.1 7.4 %final.1 = bf16[2048,512]{1,0:T(8,128)(2,1)} custom-call(bf16[2048,512]{1,0:T(8,128)(2,1)} %get-tuple-element.7.inner_ref, bf16[512,256]{1,0:T(8,128)(2,1)} %get-tuple-element.8.message_ref, bf16[2,64,512]{2,1,0:T(8,128)(2,1)} %up_ref.1, bf16[2,512,512]{2,1,0:T(8,128)(2,1)} %w_in_ref.1, bf16[2,512,512]{2,1,0:T(8,128)(2,1)} %w_out_ref.1), custom_call_target="tpu_custom_call" | custom-call | tf_op jit(solution)/shard_map/final/pallas_call | solution.py:554

commit v3 on v2

--- a/solution.py
+++ b/solution.py
@@ -116,6 +116,7 @@
     send_sem,
     recv_sem,
     load_sem,
+    meet_sem,
 ):
     me_bond = lax.axis_index("bond")
     me_atom = lax.axis_index("atom")
@@ -126,14 +127,14 @@
 
     barrier = pltpu.get_barrier_semaphore()
 
-    def greet(step, carry):
-        peer = lax.rem(me + step, peers)
-        pl.semaphore_signal(
-            barrier, inc=1, device_id=(peer // atoms, lax.rem(peer, atoms)), device_id_type=MESH
-        )
-        return carry
-
-    lax.fori_loop(1, peers, greet, 0)
+    def greet(semaphore, bond, atom):
+        pl.semaphore_signal(semaphore, inc=1, device_id=(bond, atom), device_id_type=MESH)
+
+    bonds = peers // atoms
+    for step in range(1, atoms):
+        greet(barrier, me_bond, lax.rem(me_atom + step, atoms))
+    for step in range(1, bonds):
+        greet(barrier, lax.rem(me_bond + step, bonds), me_atom)
 
     loads = [
         pltpu.make_async_copy(src, dst, load_sem.at[n])
@@ -173,6 +174,10 @@
                 pick_send[c, h * 256 + o * 32 : h * 256 + (o + 1) * 32, :] = one_hot(col & 511, pos)
 
     loop(16, 1, build_send)
+    pl.semaphore_wait(barrier, atoms + bonds - 2)
+    for step in range(1, bonds):
+        greet(meet_sem, lax.rem(me_bond + step, bonds), me_atom)
+
 
     loads[0].wait()
     for l in range(layers):
@@ -194,7 +199,7 @@
         copy.wait()
     loop(4, 1, first)
 
-    pl.semaphore_wait(barrier, peers - 1)
+    pl.semaphore_wait(meet_sem, bonds - 1)
 
     def send_block(src, dst, peer, sem_index, recv):
         @pl.when(peer != me)
@@ -528,6 +533,7 @@
             pltpu.SemaphoreType.DMA((4,)),
             pltpu.SemaphoreType.DMA((16,)),
             pltpu.SemaphoreType.DMA((10,)),
+            pltpu.SemaphoreType.REGULAR,
         ],
         compiler_params=pltpu.CompilerParams(
             collective_id=0, has_side_effects=True, vmem_limit_bytes=67043328

time: 108 us -> 107 us (level)
  no operation moved by 1% of the time
where the time goes in v3:
time: 107 us
  Pallas kernels  106 us (99%)
    pallas_call x1, Pallas kernels, on_device(): pl.pallas_call(kernel, name='triplet', out_shape=(jax.ShapeDtypeStruct((2...  99.1 us
    pallas_call x1, Pallas kernels, on_device(): pl.pallas_call(final, name='final', grid=(4,), out_shape=jax.ShapeDtypeSt...  7.37 us

profile of v3, /device:TPU:1, one launch (start us, length us, event | category | flops | bytes accessed | tf_op | source)
XLA Modules:
  0.0 107.1 jit_solution(11077637744683011836)
XLA Ops:
  0.7 99.1 %triplet.1 = (bf16[2048,512]{1,0:T(8,128)(2,1)}, bf16[512,256]{1,0:T(8,128)(2,1)}) custom-call(s32[1]{0:T(128)S(6)} %copy.15.count_ref, s32[64,128]{1,0:T(8,128)} %bitcast.11, s32[16,128]{1,0:T(8,128)} %bitcast.13, s32[16,128]{1,0:T(8,128)} %bitcast.12, s32[1,2048]{1,0:T(1,128)} %target_row_ref.1, s32[32,128]{1,0:T(8,128)} %bitcast.10, ...), custom_call_target="tpu_custom_call" | custom-call | tf_op jit(solution)/shard_map/triplet/pallas_call | solution.py:490
  99.7 7.4 %final.1 = bf16[2048,512]{1,0:T(8,128)(2,1)} custom-call(bf16[2048,512]{1,0:T(8,128)(2,1)} %get-tuple-element.7.inner_ref, bf16[512,256]{1,0:T(8,128)(2,1)} %get-tuple-element.8.message_ref, bf16[2,64,512]{2,1,0:T(8,128)(2,1)} %up_ref.1, bf16[2,512,512]{2,1,0:T(8,128)(2,1)} %w_in_ref.1, bf16[2,512,512]{2,1,0:T(8,128)(2,1)} %w_out_ref.1), custom_call_target="tpu_custom_call" | custom-call | tf_op jit(solution)/shard_map/final/pallas_call | solution.py:560
